TPU v7x, 32 devices: a whole 2x2x4 slice. The times are simulated.
32 devices in a mesh: prow: 8 (over z, y), pcol: 4 (over x, core).
Axes of the slice: x: 2, y: 2, z: 4, core: 2. Of those that a mesh axis runs over, the one named last changes fastest.
Arguments:
- inverse_tiles: bfloat16 [24576, 24576], P('prow', 'pcol'), may hold values from -6 to 6
- panel_blocks: bfloat16 [24576, 1536], P(('prow', 'pcol')), may hold values from -0.0546875 to 0.0546875
- pivot_inverse: bfloat16 [3, 512, 512], replicated, may hold values from -0.25 to 0.25
- diagonal_inverse: float32 [3, 512, 512], replicated, may hold values from -6 to 6
- ancestors: int32 [3, 24], replicated, may hold values from 0 to 47, all different within a row
Outputs:
- cross_blocks: float32 [24576, 1536], P(('prow', 'pcol'))
- diagonal_blocks: float32 [3, 512, 512], replicated
Inputs may be any that keep to these rules, and one draw needn't show every extreme that they name: `ancestors`: each row names 24 different blocks, and every block is named by some row.
All inputs are finite; a program needn't handle non-finite values.
Results may differ from a plain program's by a relative error of at most 0.003.
Values may be sent and summed in bfloat16 or wider, within the bound.
A program may use at most 128 MiB of HBM per device.

v0:
```python
import jax
import jax.numpy as jnp
from jax import lax
from jax.sharding import PartitionSpec as P


def spread(value, axis, source):
    kept = jnp.where(lax.axis_index(axis) == source, value, 0).astype(value.dtype)
    return lax.psum(kept, axis)


def row_terms(inverse_tiles, columns):
    return jnp.dot(inverse_tiles, columns, preferred_element_type=jnp.float32)


def on_device(inverse_tiles, panel_blocks, pivot_inverse, diagonal_inverse, ancestors):
    seg_rows = panel_blocks.shape[0]
    n_super = pivot_inverse.shape[0]
    width = pivot_inverse.shape[1]
    row_devices = lax.axis_size("prow")
    col_devices = lax.axis_size("pcol")
    segment = lax.axis_index("prow") * col_devices + lax.axis_index("pcol")
    row_ids = segment * seg_rows + lax.iota(jnp.int32, seg_rows)
    block_ids = row_ids // width
    listed = jnp.any(block_ids[:, None, None] == ancestors[None, :, :], axis=2).astype(jnp.float32)
    raw_three = panel_blocks.reshape(seg_rows, n_super, width)
    normed = jnp.einsum(
        "rsw,swv->rsv", raw_three, pivot_inverse, preferred_element_type=jnp.float32
    )
    scaled = (normed * listed[:, :, None]).astype(jnp.bfloat16)
    own_panel = scaled.reshape(seg_rows, n_super * width)
    row_panel = lax.all_gather(own_panel, "pcol", axis=0, tiled=True)
    ratio = row_devices // col_devices
    pieces = []
    for offset in range(ratio):
        pieces.append(spread(row_panel, "prow", lax.axis_index("pcol") * ratio + offset))
    column_panel = jnp.concatenate(pieces, axis=0)
    summed = lax.psum_scatter(
        row_terms(inverse_tiles, column_panel), "pcol", scatter_dimension=0, tiled=True
    )
    cross = -(summed.reshape(seg_rows, n_super, width) * listed[:, :, None])
    local_terms = jnp.einsum(
        "rsw,rsv->swv", scaled.astype(jnp.float32), cross, precision=lax.Precision.HIGHEST
    )
    total = lax.psum(local_terms, ("prow", "pcol"))
    diagonal = diagonal_inverse - total
    return (cross.reshape(seg_rows, n_super * width), diagonal)


def solution(mesh):
    in_specs = (P("prow", "pcol"), P(("prow", "pcol"), None), P(), P(), P())
    out_specs = (P(("prow", "pcol"), None), P())
    return jax.shard_map(
        on_device, mesh=mesh, in_specs=in_specs, out_specs=out_specs, check_vma=False
    )
```

profile of v0, /device:TPU:0, one launch (start us, length us, event | category | flops | bytes accessed | tf_op | source)
XLA Modules:
  0.0 1028.7 jit_solution(8723417123079161685)
XLA Ops:
  7.2 0.0 copy-start
  7.2 0.0 all-gather.2.cloned.1.call-start
  7.3 0.9 compare_reduce_fusion
  8.2 0.0 copy-start.2
  8.2 4.3 copy.16
  12.4 4.5 fusion.8
  17.0 0.0 all-gather.2.cloned.1.call-update
  17.0 0.0 all-reduce.6.cloned.1.call-start
  17.0 67.0 %all-gather.2.cloned.1.call-done = bf16[3072,1536]{0,1:T(8,128)(2,1)} async-done(((bf16[768,1536]{0,1:T(8,128)(2,1)}), bf16[3072,1536]{0,1:T(8,128)(2,1)}) %all-gather.2.cloned.1.call-update) | async-done | bytes 9437200 | tf_op jit(solution)/shard_map/all_gather | solution.py:32
  84.1 10.7 %broadcast_select_fusion.1 = (bf16[3072,1536]{0,1:T(8,128)(2,1)}, bf16[3072,1536]{0,1:T(8,128)(2,1)}) fusion(bf16[3072,1536]{0,1:T(8,128)(2,1)} %all-gather.2.cloned.1.call-done, pred[]{:T(512)S(6)} %eq.19, pred[]{:T(512)S(6)} %eq.23), kind=kLoop, calls=%fused_computation.6 | loop fusion | flops 9437184 | bytes 28311554 | tf_op jit(solution)/shard_map/jit(_where)/select_n | solution.py:8
  94.8 0.0 all-reduce.6.cloned.1.call-update
  94.8 0.0 reduce-scatter.2.cloned.1.call-start
  94.9 567.5 %all-reduce.6.cloned.1.call-done = (bf16[3072,1536]{0,1:T(8,128)(2,1)}, bf16[3072,1536]{0,1:T(8,128)(2,1)}) async-done(((bf16[3072,1536]{0,1:T(8,128)(2,1)}, bf16[3072,1536]{0,1:T(8,128)(2,1)}), (bf16[3072,1536]{0,1:T(8,128)(2,1)}, bf16[3072,1536]{0,1:T(8,128)(2,1)})) %all-reduce.6.cloned.1.call-update) | async-done | bytes 18874384 | tf_op jit(solution)/shard_map/psum | solution.py:9
  662.4 70.5 %fusion.4 = f32[3072,1536]{0,1:T(8,128)} fusion(bf16[3072,6144]{1,0:T(8,128)(2,1)} %param.5, bf16[3072,1536]{0,1:T(8,128)(2,1)} %get-tuple-element.8, bf16[3072,1536]{0,1:T(8,128)(2,1)} %get-tuple-element.9), kind=kOutput, calls=%fused_computation.4 | convolution fusion | flops 58019807232 | bytes 75497472 | tf_op jit(solution)/shard_map/dot_general | solution.py:13
  732.9 0.0 reduce-scatter.2.cloned.1.call-update
  732.9 0.2 all-reduce.4.cloned.1.call-start
  733.2 136.7 %reduce-scatter.2.cloned.1.call-done = f32[768,1536]{0,1:T(8,128)} async-done(((f32[3072,1536]{0,1:T(8,128)}), f32[768,1536]{0,1:T(8,128)}) %reduce-scatter.2.cloned.1.call-update) | async-done | bytes 4718608 | tf_op jit(solution)/shard_map/reduce_scatter | solution.py:38
  869.8 8.8 fusion.9
  878.6 0.0 all-reduce.4.cloned.1.call-update
  878.6 4.8 fusion.7
  883.4 6.4 copy.20
  889.9 127.0 %all-reduce.4.cloned.1.call-done = f32[3,512,512]{2,1,0:T(8,128)} async-done(((f32[3,512,512]{2,1,0:T(8,128)}), f32[3,512,512]{2,1,0:T(8,128)}) %all-reduce.4.cloned.1.call-update) | async-done | bytes 3145744 | tf_op jit(solution)/shard_map/psum | solution.py:45
  1016.9 5.3 sub.10
  1022.2 0.0 copy-done.1
  (7 shorter events, 0.0 us)
Async XLA Ops:
  7.2 5.3 copy-start
  7.2 76.9 %all-gather.2.cloned.1.call-start = ((), (), s32[]{:S(2)}) async-start(), calls=%async_computation.1 | async-start | bytes 11796480 | tf_op jit(solution)/shard_map/all_gather | solution.py:32
  8.2 8.8 copy-start.2
  17.0 645.4 %all-reduce.6.cloned.1.call-start = ((), (), s32[]{:S(2)}) async-start(), calls=%async_computation.4 | async-start | bytes 37748736 | tf_op jit(solution)/shard_map/psum | solution.py:9
  94.8 775.0 %reduce-scatter.2.cloned.1.call-start = ((), (), s32[]{:S(2)}) async-start(), calls=%async_computation.2 | async-start | bytes 23592960 | tf_op jit(solution)/shard_map/reduce_scatter | solution.py:38
  732.9 136.9 %copy-start.3 = (f32[768,3]{0,1:T(4,128)S(1)}, f32[768,3]{0,1:T(4,128)}, u32[]{:S(2)}) copy-start(f32[768,3]{0,1:T(4,128)} %copy-done.2) | copy-start | bytes 27652
  732.9 284.0 %all-reduce.4.cloned.1.call-start = ((), (), s32[]{:S(2)}) async-start(), calls=%async_computation.3 | async-start | bytes 6291456 | tf_op jit(solution)/shard_map/psum | solution.py:45
  883.4 138.7 %copy-start.1 = (bf16[3,512,512]{2,1,0:T(8,128)(2,1)S(1)}, bf16[3,512,512]{2,1,0:T(8,128)(2,1)}, u32[]{:S(2)}) copy-start(bf16[3,512,512]{2,1,0:T(8,128)(2,1)} %param.7) | copy-start | bytes 4718596
Sparse Core Ops, SparseCore 0:
  17.1 66.9 all-gather.1
  94.9 567.4 all-reduce.5
  733.0 136.7 reduce-scatter.1
  878.8 138.0 all-reduce.3
where the time goes:
time: 1030 us
  waiting for transfers between devices  898 us (87%)
  matrix products  83.8 us (8%)
  other arithmetic  21.7 us (2%)
  between operations  13.8 us (1%)
  local copies, waits for them, and re-layouts  10.7 us (1%)
    psum x1, waiting for transfers between devices, spread(): return lax.psum(kept, axis)  568 us
    reduce_scatter x1, waiting for transfers between devices, on_device(): lax.psum_scatter(row_terms(inverse_tiles, column_panel), 'pcol', scatter_...  137 us
    psum x1, waiting for transfers between devices, on_device(): total = lax.psum(local_terms, ('prow', 'pcol'))  127 us
    dot_general x1, matrix products, row_terms(): return jnp.dot(inverse_tiles, columns, preferred_element_type=jnp.float32)  70.5 us
    all_gather x1, waiting for transfers between devices, on_device(): row_panel = lax.all_gather(own_panel, 'pcol', axis=0, tiled=True)  67 us
  transfers between devices with their start and end apart: 4, of which 4 were waited for; matrix products, arithmetic and copies ran while one was open for 1% of the time, Pallas kernels for 0%

commit v1 on v0

v1 whole, which is shorter than its diff:
```python
import jax
import jax.numpy as jnp
from jax import lax
from jax.sharding import PartitionSpec as P


def reduce_rows(partial, seg_rows):
    devices = lax.axis_size("pcol")
    width = partial.shape[1]
    me = lax.axis_index("pcol")
    if devices & (devices - 1):
        return lax.psum_scatter(partial, "pcol", scatter_dimension=0, tiled=True)
    value = partial.reshape(devices, seg_rows, width)
    bit = 1
    while bit < devices:
        mine = (me // bit) % 2
        halves = value.reshape(value.shape[0] // 2, 2, seg_rows, width)
        keep = jnp.where(mine == 0, halves[:, 0], halves[:, 1])
        send = jnp.where(mine == 0, halves[:, 1], halves[:, 0]).astype(jnp.bfloat16)
        got = lax.ppermute(send, "pcol", [(d, d ^ bit) for d in range(devices)])
        value = keep + got.astype(jnp.float32)
        bit *= 2
    return value.reshape(seg_rows, width)


def on_device(inverse_tiles, panel_blocks, pivot_inverse, diagonal_inverse, ancestors):
    seg_rows = panel_blocks.shape[0]
    n_super = pivot_inverse.shape[0]
    width = pivot_inverse.shape[1]
    row_devices = lax.axis_size("prow")
    col_devices = lax.axis_size("pcol")
    segment = lax.axis_index("prow") * col_devices + lax.axis_index("pcol")
    row_ids = segment * seg_rows + lax.iota(jnp.int32, seg_rows)
    block_ids = row_ids // width
    listed = jnp.any(block_ids[:, None, None] == ancestors[None, :, :], axis=2).astype(jnp.float32)
    route = []
    for s in range(row_devices * col_devices):
        route.append((s, (s % row_devices) * col_devices + s // row_devices))
    crosses, terms = [], []
    scaled, panels = [], []
    for k in range(n_super):
        normed = jnp.dot(
            panel_blocks[:, k * width:(k + 1) * width], pivot_inverse[k],
            preferred_element_type=jnp.float32,
        )
        own = (normed * listed[:, k:k + 1]).astype(jnp.bfloat16)
        scaled.append(own)
        moved = lax.ppermute(own, ("prow", "pcol"), route)
        panels.append(lax.all_gather(moved, "prow", axis=0, tiled=True))
    for k in range(n_super):
        product = jnp.dot(inverse_tiles, panels[k], preferred_element_type=jnp.float32)
        summed = reduce_rows(product, seg_rows)
        cross = -(summed * listed[:, k:k + 1])
        crosses.append(cross)
        term = lax.dot_general(
            scaled[k].astype(jnp.float32), cross, (((0,), (0,)), ((), ())),
            precision=lax.Precision.HIGHEST,
        )
        if terms:
            term, terms[-1] = lax.optimization_barrier((term, terms[-1]))
        terms.append(lax.psum(term, ("prow", "pcol")))
    diagonal = diagonal_inverse - jnp.stack(terms)
    return (jnp.concatenate(crosses, axis=1), diagonal)


def solution(mesh):
    in_specs = (P("prow", "pcol"), P(("prow", "pcol"), None), P(), P(), P())
    out_specs = (P(("prow", "pcol"), None), P())
    return jax.shard_map(
        on_device, mesh=mesh, in_specs=in_specs, out_specs=out_specs, check_vma=False
    )
```

time: 1030 us -> 931 us (0.904)
  waiting for transfers between devices: 898 us -> 749 us
  local copies, waits for them, and re-layouts: 10.7 us -> 28.6 us
  other arithmetic: 21.7 us -> 38.7 us
    psum x2 -> x3, waiting for transfers between devices: 695 us -> 369 us  [on_device(): terms.append(lax.psum(term, ('prow', 'pcol')))]
    all_gather x1 -> x3, waiting for transfers between devices: 67 us -> 356 us  [on_device(): panels.append(lax.all_gather(moved, 'prow', axis=0, tiled=True))]
    reduce_scatter x1 -> x0, waiting for transfers between devices: 137 us -> none  [on_device(): lax.psum_scatter(row_terms(inverse_tiles, column_panel), 'pcol', scatter_...]
    ppermute x0 -> x9, waiting for transfers between devices: none -> 24 us  [the longest x6 24 us: reduce_rows(): got = lax.ppermute(send, 'pcol', [(d, d ^ bit) for d in range(devices)])]
    dot_general x0 -> x3, local copies, waits for them, and re-layouts: none -> 19.8 us  [on_device(): jnp.dot(inverse_tiles, panels[k], preferred_element_type=jnp.float32)]
    convert_element_type x0 -> x6, other arithmetic: none -> 15.2 us  [reduce_rows(): send = jnp.where(mine == 0, halves[:, 1], halves[:, 0]).astype(jnp.bfloat16)]
    select_n x1 -> x0, other arithmetic: 10.7 us -> none  [spread(): jnp.where(lax.axis_index(axis) == source, value, 0).astype(value.dtype)]
    dot_general x3 -> x9, matrix products: 83.8 us -> 93.5 us  [the longest x3 81 us: on_device(): jnp.dot(inverse_tiles, panels[k], preferred_element_type=jnp.float32)]
  transfers between devices with their start and end apart: 4 -> 15, of which waited for: 4 -> 8; matrix products, arithmetic and copies ran while one was open for 1% -> 15% of each run, Pallas kernels for 0% -> 0%
where the time goes in v1:
time: 931 us
  waiting for transfers between devices  749 us (80%)
  matrix products  93.5 us (10%)
  other arithmetic  38.7 us (4%)
  local copies, waits for them, and re-layouts  28.6 us (3%)
  between operations  14.5 us (2%)
    psum x3, waiting for transfers between devices, on_device(): terms.append(lax.psum(term, ('prow', 'pcol')))  369 us
    all_gather x3, waiting for transfers between devices, on_device(): panels.append(lax.all_gather(moved, 'prow', axis=0, tiled=True))  356 us
    dot_general x3, matrix products, on_device(): jnp.dot(inverse_tiles, panels[k], preferred_element_type=jnp.float32)  81 us
    ppermute x6, waiting for transfers between devices, reduce_rows(): got = lax.ppermute(send, 'pcol', [(d, d ^ bit) for d in range(devices)])  24 us
    dot_general x3, local copies, waits for them, and re-layouts, on_device(): jnp.dot(inverse_tiles, panels[k], preferred_element_type=jnp.float32)  19.8 us
  transfers between devices with their start and end apart: 15, of which 8 were waited for; matrix products, arithmetic and copies ran while one was open for 15% of the time, Pallas kernels for 0%

profile of v1, /device:TPU:0, one launch (start us, length us, event | category | flops | bytes accessed | tf_op | source)
XLA Modules:
  0.0 930.5 jit_solution(15570290861522427411)
XLA Ops:
  21.1 231.4 %all-gather.6.cloned.1.call-done = bf16[6144,512]{1,0:T(8,128)(2,1)} async-done(((bf16[768,512]{1,0:T(8,128)(2,1)}), bf16[6144,512]{1,0:T(8,128)(2,1)}) %all-gather.6.cloned.1.call-update) | async-done | bytes 6291472 | tf_op jit(solution)/shard_map/all_gather | solution.py:49
  252.5 27.0 %convolution_bitcast_fusion.1 = f32[3072,512]{0,1:T(8,128)} fusion(bf16[6144,512]{1,0:T(8,128)(2,1)} %all-gather.6.cloned.1.call-done, bf16[3072,6144]{1,0:T(8,128)(2,1)} %param.5), kind=kOutput, calls=%fused_computation.1 | convolution fusion | flops 19327352832 | bytes 50331648 | tf_op jit(solution)/shard_map/dot_general | solution.py:51
  279.5 6.6 copy.19
  286.1 4.3 fusion.4
  290.4 63.0 %all-gather.4.cloned.1.call-done = bf16[6144,512]{1,0:T(8,128)(2,1)} async-done(((bf16[768,512]{1,0:T(8,128)(2,1)}), bf16[6144,512]{1,0:T(8,128)(2,1)}) %all-gather.4.cloned.1.call-update) | async-done | bytes 6291472 | tf_op jit(solution)/shard_map/all_gather | solution.py:49
  353.4 27.0 %convolution_bitcast_fusion.2 = f32[3072,512]{0,1:T(8,128)} fusion(bf16[6144,512]{1,0:T(8,128)(2,1)} %all-gather.4.cloned.1.call-done, bf16[3072,6144]{1,0:T(8,128)(2,1)} %param.5), kind=kOutput, calls=%fused_computation.2 | convolution fusion | flops 19327352832 | bytes 50331648 | tf_op jit(solution)/shard_map/dot_general | solution.py:51
  380.4 6.6 copy.16
  386.9 4.4 fusion.3
  391.3 61.8 %all-gather.8.cloned.1.call-done = bf16[6144,512]{1,0:T(8,128)(2,1)} async-done(((bf16[768,512]{1,0:T(8,128)(2,1)}), bf16[6144,512]{1,0:T(8,128)(2,1)}) %all-gather.8.cloned.1.call-update) | async-done | bytes 6291472 | tf_op jit(solution)/shard_map/all_gather | solution.py:49
  453.1 27.0 %convolution_bitcast_fusion = f32[3072,512]{0,1:T(8,128)} fusion(bf16[6144,512]{1,0:T(8,128)(2,1)} %all-gather.8.cloned.1.call-done, bf16[3072,6144]{1,0:T(8,128)(2,1)} %param.5), kind=kOutput, calls=%fused_computation | convolution fusion | flops 19327352832 | bytes 50331648 | tf_op jit(solution)/shard_map/dot_general | solution.py:51
  480.1 6.6 copy.22
  486.7 4.3 fusion.5
  490.9 4.4 fusion.2
  506.1 9.9 %collective-permute-done.2 = bf16[1,768,512]{2,1,0:T(8,128)(2,1)S(1)} collective-permute-done((bf16[1,768,512]{2,1,0:T(8,128)(2,1)S(1)}, bf16[1,768,512]{2,1,0:T(8,128)(2,1)S(1)}, u32[]{:S(2)}, u32[]{:S(2)}) %collective-permute-start.2) | collective-permute-done | bytes 786464 | tf_op jit(solution)/shard_map/ppermute | solution.py:20
  517.5 2.5 fusion.25
  520.3 14.1 %collective-permute-done.5 = bf16[1,768,512]{2,1,0:T(8,128)(2,1)} collective-permute-done((bf16[1,768,512]{2,1,0:T(8,128)(2,1)}, bf16[1,768,512]{2,1,0:T(8,128)(2,1)}, u32[]{:S(2)}, u32[]{:S(2)}) %collective-permute-start.5) | collective-permute-done | bytes 786464 | tf_op jit(solution)/shard_map/ppermute | solution.py:20
  534.3 2.4 fusion.7
  537.9 2.5 fusion.24
  540.4 108.7 %all-reduce.4.cloned.1.call-done = f32[512,512]{1,0:T(8,128)} async-done(((f32[512,512]{1,0:T(8,128)}), f32[512,512]{1,0:T(8,128)}) %all-reduce.4.cloned.1.call-update) | async-done | bytes 1048592 | tf_op jit(solution)/shard_map/psum | solution.py:61
  651.8 2.5 fusion.26
  654.3 129.4 %all-reduce.6.cloned.1.call-done = f32[512,512]{1,0:T(8,128)} async-done(((f32[512,512]{1,0:T(8,128)}), f32[512,512]{1,0:T(8,128)}) %all-reduce.6.cloned.1.call-update) | async-done | bytes 1048592 | tf_op jit(solution)/shard_map/psum | solution.py:61
  783.8 3.9 pad_maximum_fusion
  787.7 130.7 %all-reduce.8.cloned.1.call-done = f32[1,512,512]{2,1,0:T(8,128)} async-done(((f32[1,512,512]{2,1,0:T(8,128)}), f32[1,512,512]{2,1,0:T(8,128)}) %all-reduce.8.cloned.1.call-update) | async-done | bytes 1048592 | tf_op jit(solution)/shard_map/psum | solution.py:61
  918.5 5.2 maximum_subtract_fusion
  (84 shorter events, 30.0 us)
Async XLA Ops:
  7.2 5.5 copy-start.15
  7.2 245.3 %all-gather.6.cloned.1.call-start = ((), (), s32[]{:S(2)}) async-start(), calls=%async_computation.1 | async-start | bytes 7077888 | tf_op jit(solution)/shard_map/all_gather | solution.py:49
  11.0 0.7 collective-permute-start.3
  12.6 340.7 %all-gather.4.cloned.1.call-start = ((), (), s32[]{:S(2)}) async-start(), calls=%async_computation | async-start | bytes 7077888 | tf_op jit(solution)/shard_map/all_gather | solution.py:49
  15.2 0.7 collective-permute-start
  16.8 436.3 %all-gather.8.cloned.1.call-start = ((), (), s32[]{:S(2)}) async-start(), calls=%async_computation.2 | async-start | bytes 7077888 | tf_op jit(solution)/shard_map/all_gather | solution.py:49
  19.4 0.7 collective-permute-start.6
  21.0 628.1 %all-reduce.4.cloned.1.call-start = ((), (), s32[]{:S(2)}) async-start(), calls=%async_computation.3 | async-start | bytes 2097152 | tf_op jit(solution)/shard_map/psum | solution.py:61
  290.4 206.7 %collective-permute-start.4 = (bf16[2,768,512]{2,1,0:T(8,128)(2,1)}, bf16[2,768,512]{2,1,0:T(8,128)(2,1)}, u32[]{:S(2)}, u32[]{:S(2)}) collective-permute-start(bf16[2,768,512]{2,1,0:T(8,128)(2,1)} %fusion.4), channel_id=1, source_target_pairs={{0,1},{1,0},{2,3},{3,2},{4,5},{5,4},{6,7},{7,6},{8,9},{9,8},{10,11... | collective-permute-start | bytes 4718600 | tf_op jit(solution)/shard_map/ppermute | solution.py:20
  391.3 99.6 %collective-permute-start.1 = (bf16[2,768,512]{2,1,0:T(8,128)(2,1)}, bf16[2,768,512]{2,1,0:T(8,128)(2,1)}, u32[]{:S(2)}, u32[]{:S(2)}) collective-permute-start(bf16[2,768,512]{2,1,0:T(8,128)(2,1)} %fusion.3), channel_id=1, source_target_pairs={{0,1},{1,0},{2,3},{3,2},{4,5},{5,4},{6,7},{7,6},{8,9},{9,8},{10,11... | collective-permute-start | bytes 4718600 | tf_op jit(solution)/shard_map/ppermute | solution.py:20
  490.9 10.5 %collective-permute-start.7 = (bf16[2,768,512]{2,1,0:T(8,128)(2,1)}, bf16[2,768,512]{2,1,0:T(8,128)(2,1)}, u32[]{:S(2)}, u32[]{:S(2)}) collective-permute-start(bf16[2,768,512]{2,1,0:T(8,128)(2,1)} %fusion.5), channel_id=1, source_target_pairs={{0,1},{1,0},{2,3},{3,2},{4,5},{5,4},{6,7},{7,6},{8,9},{9,8},{10,11... | collective-permute-start | bytes 4718600 | tf_op jit(solution)/shard_map/ppermute | solution.py:20
  490.9 6.1 slice-start
  490.9 6.1 slice-start.1
  495.3 6.1 slice-start.2
  495.5 6.0 slice-start.3
  495.5 20.5 %collective-permute-start.2 = (bf16[1,768,512]{2,1,0:T(8,128)(2,1)S(1)}, bf16[1,768,512]{2,1,0:T(8,128)(2,1)S(1)}, u32[]{:S(2)}, u32[]{:S(2)}) collective-permute-start(bf16[1,768,512]{2,1,0:T(8,128)(2,1)S(1)} %fusion.9), channel_id=1, source_target_pairs={{0,2},{1,3},{2,0},{3,1},{4,6},{5,7},{6,4},{7,5},{8,10},{9,11},{10,... | collective-permute-start | bytes 2359304 | tf_op jit(solution)/shard_map/ppermute | solution.py:20
  500.6 33.7 %collective-permute-start.5 = (bf16[1,768,512]{2,1,0:T(8,128)(2,1)}, bf16[1,768,512]{2,1,0:T(8,128)(2,1)}, u32[]{:S(2)}, u32[]{:S(2)}) collective-permute-start(bf16[1,768,512]{2,1,0:T(8,128)(2,1)} %fusion.10), channel_id=1, source_target_pairs={{0,2},{1,3},{2,0},{3,1},{4,6},{5,7},{6,4},{7,5},{8,10},{9,11},{10,... | collective-permute-start | bytes 2359304 | tf_op jit(solution)/shard_map/ppermute | solution.py:20
  504.9 12.6 %copy-start.14 = (bf16[768,512]{1,0:T(8,128)(2,1)S(1)}, bf16[768,512]{1,0:T(8,128)(2,1)}, u32[]{:S(2)}) copy-start(bf16[768,512]{1,0:T(8,128)(2,1)} %copy-done.13) | copy-start | bytes 2359300
  504.9 144.2 %collective-permute-start.8 = (bf16[1,768,512]{2,1,0:T(8,128)(2,1)}, bf16[1,768,512]{2,1,0:T(8,128)(2,1)}, u32[]{:S(2)}, u32[]{:S(2)}) collective-permute-start(bf16[1,768,512]{2,1,0:T(8,128)(2,1)} %fusion.11), channel_id=1, source_target_pairs={{0,2},{1,3},{2,0},{3,1},{4,6},{5,7},{6,4},{7,5},{8,10},{9,11},{10,... | collective-permute-start | bytes 2359304 | tf_op jit(solution)/shard_map/ppermute | solution.py:20
  520.0 263.8 %all-reduce.6.cloned.1.call-start = ((), (), s32[]{:S(2)}) async-start(), calls=%async_computation.4 | async-start | bytes 2097152 | tf_op jit(solution)/shard_map/psum | solution.py:61
  520.3 17.7 %copy-start.10 = (bf16[768,512]{1,0:T(8,128)(2,1)S(1)}, bf16[768,512]{1,0:T(8,128)(2,1)}, u32[]{:S(2)}) copy-start(bf16[768,512]{1,0:T(8,128)(2,1)} %copy-done.9) | copy-start | bytes 2359300
  649.1 269.4 %all-reduce.8.cloned.1.call-start = ((), (), s32[]{:S(2)}) async-start(), calls=%async_computation.5 | async-start | bytes 2097152 | tf_op jit(solution)/shard_map/psum | solution.py:61
  651.8 132.0 %copy-start.2 = (f32[768,512]{1,0:T(8,128)S(1)}, f32[768,512]{1,0:T(8,128)}, u32[]{:S(2)}) copy-start(f32[768,512]{1,0:T(8,128)} %copy-done.1) | copy-start | bytes 4718596
  651.8 132.0 %copy-start.4 = (f32[768,512]{1,0:T(8,128)S(1)}, f32[768,512]{1,0:T(8,128)}, u32[]{:S(2)}) copy-start(f32[768,512]{1,0:T(8,128)} %copy-done.3) | copy-start | bytes 4718596
  (11 other events, 15.9 us)
Sparse Core Ops, SparseCore 0:
  12.7 239.7 all-gather.5
  254.7 98.6 all-gather.3
  356.1 96.9 all-gather.7
  520.1 128.9 all-reduce.3
  654.1 129.6 all-reduce.5
  788.8 129.6 all-reduce.7

commit v2 on v1

--- a/solution.py
+++ b/solution.py
@@ -23,6 +23,35 @@
     return value.reshape(seg_rows, width)
 
 
+def sum_everywhere(terms):
+    axes = ("prow", "pcol")
+    devices = lax.axis_size("prow") * lax.axis_size("pcol")
+    rows = terms.shape[0] * terms.shape[1]
+    if devices & (devices - 1) or rows % devices:
+        return lax.psum(terms, axes)
+    me = lax.axis_index("prow") * lax.axis_size("pcol") + lax.axis_index("pcol")
+    value = terms.reshape(rows, terms.shape[2])
+    bits = []
+    bit = 1
+    while bit < devices:
+        bits.append(bit)
+        bit *= 2
+    for bit in bits:
+        low = (me // bit) % 2 == 0
+        half = value.shape[0] // 2
+        keep = jnp.where(low, value[:half], value[half:])
+        send = jnp.where(low, value[half:], value[:half])
+        value = keep + lax.ppermute(send, axes, [(d, d ^ bit) for d in range(devices)])
+    value = value.astype(jnp.bfloat16)
+    for bit in reversed(bits):
+        low = (me // bit) % 2 == 0
+        got = lax.ppermute(value, axes, [(d, d ^ bit) for d in range(devices)])
+        value = jnp.concatenate(
+            [jnp.where(low, value, got), jnp.where(low, got, value)], axis=0
+        )
+    return value.astype(jnp.float32).reshape(terms.shape)
+
+
 def on_device(inverse_tiles, panel_blocks, pivot_inverse, diagonal_inverse, ancestors):
     seg_rows = panel_blocks.shape[0]
     n_super = pivot_inverse.shape[0]
@@ -45,10 +74,20 @@
         )
         own = (normed * listed[:, k:k + 1]).astype(jnp.bfloat16)
         scaled.append(own)
+        if k == 0:
+            whole = lax.all_gather(own, ("prow", "pcol"), axis=0, tiled=True)
+            rows = inverse_tiles.shape[1]
+            panels.append(lax.dynamic_slice_in_dim(whole, lax.axis_index("pcol") * rows, rows, 0))
+            continue
+        if k > 1:
+            own, _ = lax.optimization_barrier((own, moved))
         moved = lax.ppermute(own, ("prow", "pcol"), route)
         panels.append(lax.all_gather(moved, "prow", axis=0, tiled=True))
     for k in range(n_super):
-        product = jnp.dot(inverse_tiles, panels[k], preferred_element_type=jnp.float32)
+        panel = panels[k]
+        if k:
+            panel, terms[-1] = lax.optimization_barrier((panel, terms[-1]))
+        product = jnp.dot(inverse_tiles, panel, preferred_element_type=jnp.float32)
         summed = reduce_rows(product, seg_rows)
         cross = -(summed * listed[:, k:k + 1])
         crosses.append(cross)
@@ -56,10 +95,8 @@
             scaled[k].astype(jnp.float32), cross, (((0,), (0,)), ((), ())),
             precision=lax.Precision.HIGHEST,
         )
-        if terms:
-            term, terms[-1] = lax.optimization_barrier((term, terms[-1]))
-        terms.append(lax.psum(term, ("prow", "pcol")))
-    diagonal = diagonal_inverse - jnp.stack(terms)
+        terms.append(term)
+    diagonal = diagonal_inverse - sum_everywhere(jnp.stack(terms))
     return (jnp.concatenate(crosses, axis=1), diagonal)
 
 

time: 931 us -> 612 us (0.66)
  waiting for transfers between devices: 749 us -> 333 us
  starting transfers between devices: 6.1 us -> 105 us
    psum x3 -> x0, waiting for transfers between devices: 369 us -> none  [on_device(): terms.append(lax.psum(term, ('prow', 'pcol')))]
    all_gather x3 -> x2, waiting for transfers between devices: 356 us -> 25.3 us  [on_device(): panels.append(lax.all_gather(moved, 'prow', axis=0, tiled=True))]
    all_gather x0 -> x1, waiting for transfers between devices: none -> 191 us  [on_device(): whole = lax.all_gather(own, ('prow', 'pcol'), axis=0, tiled=True)]
    ppermute x6, starting transfers between devices: 3.54 us -> 95.3 us  [reduce_rows(): got = lax.ppermute(send, 'pcol', [(d, d ^ bit) for d in range(devices)])]
    ppermute x0 -> x10, waiting for transfers between devices: none -> 63 us  [the longest x5 42.5 us: sum_everywhere(): lax.ppermute(send, axes, [(d, d ^ bit) for d in range(devices)])]
    ppermute x6, waiting for transfers between devices: 24 us -> 53.7 us  [reduce_rows(): got = lax.ppermute(send, 'pcol', [(d, d ^ bit) for d in range(devices)])]
  transfers between devices with their start and end apart: 15 -> 21, of which waited for: 8 -> 17; matrix products, arithmetic and copies ran while one was open for 15% -> 15% of each run, Pallas kernels for 0% -> 0%
where the time goes in v2:
time: 612 us; the launch traced here: 611 us
  waiting for transfers between devices  333 us (54%)
  starting transfers between devices  105 us (17%)
  matrix products  94 us (15%)
  other arithmetic  36.9 us (6%)
  local copies, waits for them, and re-layouts  28.3 us (5%)
  between operations  14.2 us (2%)
    all_gather x1, waiting for transfers between devices, on_device(): whole = lax.all_gather(own, ('prow', 'pcol'), axis=0, tiled=True)  191 us
    ppermute x6, starting transfers between devices, reduce_rows(): got = lax.ppermute(send, 'pcol', [(d, d ^ bit) for d in range(devices)])  95.3 us
    dot_general x3, matrix products, on_device(): product = jnp.dot(inverse_tiles, panel, preferred_element_type=jnp.float32)  81.1 us
    ppermute x6, waiting for transfers between devices, reduce_rows(): got = lax.ppermute(send, 'pcol', [(d, d ^ bit) for d in range(devices)])  53.7 us
    ppermute x5, waiting for transfers between devices, sum_everywhere(): lax.ppermute(send, axes, [(d, d ^ bit) for d in range(devices)])  42.5 us
    all_gather x2, waiting for transfers between devices, on_device(): panels.append(lax.all_gather(moved, 'prow', axis=0, tiled=True))  25.3 us
    ppermute x5, waiting for transfers between devices, sum_everywhere(): got = lax.ppermute(value, axes, [(d, d ^ bit) for d in range(devices)])  20.5 us
    dot_general x3, local copies, waits for them, and re-layouts, on_device(): product = jnp.dot(inverse_tiles, panel, preferred_element_type=jnp.float32)  19.8 us
  transfers between devices with their start and end apart: 21, of which 17 were waited for; matrix products, arithmetic and copies ran while one was open for 15% of the time, Pallas kernels for 0%

profile of v2, /device:TPU:0, one launch (start us, length us, event | category | flops | bytes accessed | tf_op | source)
XLA Modules:
  0.0 611.1 jit_solution(17257424181068906410)
XLA Ops:
  15.4 190.6 %all-gather.4.cloned.1.call-done = bf16[24576,512]{1,0:T(8,128)(2,1)} async-done(((bf16[768,512]{1,0:T(8,128)(2,1)}), bf16[24576,512]{1,0:T(8,128)(2,1)}) %all-gather.4.cloned.1.call-update) | async-done | bytes 25165840 | tf_op jit(solution)/shard_map/all_gather | solution.py:78
  206.0 27.1 %fusion.2 = f32[3072,512]{0,1:T(8,128)} fusion(bf16[3072,6144]{1,0:T(8,128)(2,1)} %param.5, bf16[24576,512]{1,0:T(8,128)(2,1)} %all-gather.4.cloned.1.call-done, s32[]{:T(128)S(6)} %select_n.332), kind=kOutput, calls=%fused_computation.2 | convolution fusion | flops 19327352832 | bytes 50331652 | tf_op jit(solution)/shard_map/dot_general | solution.py:90
  233.0 6.6 %copy.16 = f32[3072,512]{1,0:T(8,128)} copy(f32[3072,512]{0,1:T(8,128)} %fusion.2) | data formatting | bytes 12582912 | tf_op jit(solution)/shard_map/dot_general | solution.py:90
  247.4 4.4 fusion.7
  252.0 82.5 %collective-permute-start.1 = (bf16[1,768,512]{2,1,0:T(8,128)(2,1)S(1)}, bf16[1,768,512]{2,1,0:T(8,128)(2,1)S(1)}, u32[]{:S(2)}, u32[]{:S(2)}) collective-permute-start(bf16[1,768,512]{2,1,0:T(8,128)(2,1)S(1)} %fusion.14), channel_id=1, source_target_pairs={{0,2},{1,3},{2,0},{3,1},{4,6},{5,7},{6,4},{7,5},{8,10},{9,11},{10,... | collective-permute-start | bytes 2359304 | tf_op jit(solution)/shard_map/ppermute | solution.py:20
  334.5 10.0 %collective-permute-done.1 = bf16[1,768,512]{2,1,0:T(8,128)(2,1)S(1)} collective-permute-done((bf16[1,768,512]{2,1,0:T(8,128)(2,1)S(1)}, bf16[1,768,512]{2,1,0:T(8,128)(2,1)S(1)}, u32[]{:S(2)}, u32[]{:S(2)}) %collective-permute-start.1) | collective-permute-done | bytes 786464 | tf_op jit(solution)/shard_map/ppermute | solution.py:20
  348.4 4.4 all-gather.6.cloned.1.call-done
  352.8 27.0 %convolution_bitcast_fusion.1 = f32[3072,512]{0,1:T(8,128)} fusion(bf16[6144,512]{1,0:T(8,128)(2,1)} %all-gather.6.cloned.1.call-done, bf16[3072,6144]{1,0:T(8,128)(2,1)} %param.5), kind=kOutput, calls=%fused_computation.4 | convolution fusion | flops 19327352832 | bytes 50331648 | tf_op jit(solution)/shard_map/dot_general | solution.py:90
  379.8 6.6 %copy.19 = f32[3072,512]{1,0:T(8,128)} copy(f32[3072,512]{0,1:T(8,128)} %convolution_bitcast_fusion.1) | data formatting | bytes 12582912 | tf_op jit(solution)/shard_map/dot_general | solution.py:90
  389.5 10.0 %collective-permute-start.3 = (bf16[2,768,512]{2,1,0:T(8,128)(2,1)S(1)}, bf16[2,768,512]{2,1,0:T(8,128)(2,1)S(1)}, u32[]{:S(2)}, u32[]{:S(2)}) collective-permute-start(bf16[2,768,512]{2,1,0:T(8,128)(2,1)S(1)} %fusion.9), channel_id=1, source_target_pairs={{0,1},{1,0},{2,3},{3,2},{4,5},{5,4},{6,7},{7,6},{8,9},{9,8},{10,11... | collective-permute-start | bytes 4718600 | tf_op jit(solution)/shard_map/ppermute | solution.py:20
  402.5 3.9 fusion.6
  407.5 18.9 %collective-permute-done.4 = bf16[1,768,512]{2,1,0:T(8,128)(2,1)S(1)} collective-permute-done((bf16[1,768,512]{2,1,0:T(8,128)(2,1)S(1)}, bf16[1,768,512]{2,1,0:T(8,128)(2,1)S(1)}, u32[]{:S(2)}, u32[]{:S(2)}) %collective-permute-start.4) | collective-permute-done | bytes 786464 | tf_op jit(solution)/shard_map/ppermute | solution.py:20
  430.4 20.9 %all-gather.8.cloned.1.call-done = bf16[6144,512]{1,0:T(8,128)(2,1)} async-done(((bf16[768,512]{1,0:T(8,128)(2,1)}), bf16[6144,512]{1,0:T(8,128)(2,1)}) %all-gather.8.cloned.1.call-update) | async-done | bytes 6291472 | tf_op jit(solution)/shard_map/all_gather | solution.py:85
  451.3 27.0 %convolution_bitcast_fusion = f32[3072,512]{0,1:T(8,128)} fusion(bf16[6144,512]{1,0:T(8,128)(2,1)} %all-gather.8.cloned.1.call-done, bf16[3072,6144]{1,0:T(8,128)(2,1)} %param.5), kind=kOutput, calls=%fused_computation.3 | convolution fusion | flops 19327352832 | bytes 50331648 | tf_op jit(solution)/shard_map/dot_general | solution.py:90
  478.3 6.6 %copy.22 = f32[3072,512]{1,0:T(8,128)} copy(f32[3072,512]{0,1:T(8,128)} %convolution_bitcast_fusion) | data formatting | bytes 12582912 | tf_op jit(solution)/shard_map/dot_general | solution.py:90
  497.8 18.4 %collective-permute-done.7 = bf16[1,768,512]{2,1,0:T(8,128)(2,1)} collective-permute-done((bf16[1,768,512]{2,1,0:T(8,128)(2,1)}, bf16[1,768,512]{2,1,0:T(8,128)(2,1)}, u32[]{:S(2)}, u32[]{:S(2)}) %collective-permute-start.7) | collective-permute-done | bytes 786464 | tf_op jit(solution)/shard_map/ppermute | solution.py:20
  530.2 18.1 %collective-permute-done.9 = f32[384,512]{1,0:T(8,128)S(1)} collective-permute-done((f32[384,512]{1,0:T(8,128)S(1)}, f32[384,512]{1,0:T(8,128)S(1)}, u32[]{:S(2)}, u32[]{:S(2)}) %collective-permute-start.9) | collective-permute-done | bytes 786464 | tf_op jit(solution)/shard_map/ppermute | solution.py:44
  550.6 9.7 %collective-permute-done.10 = f32[192,512]{1,0:T(8,128)S(1)} collective-permute-done((f32[192,512]{1,0:T(8,128)S(1)}, f32[192,512]{1,0:T(8,128)S(1)}, u32[]{:S(2)}, u32[]{:S(2)}) %collective-permute-start.10) | collective-permute-done | bytes 393248 | tf_op jit(solution)/shard_map/ppermute | solution.py:44
  560.9 5.4 collective-permute-done.11
  568.1 5.6 collective-permute-done.12
  574.3 4.5 collective-permute-done.13
  578.9 4.6 collective-permute-done.14
  584.2 5.1 collective-permute-done.15
  591.0 6.3 %collective-permute-done.16 = bf16[384,512]{1,0:T(8,128)(2,1)S(1)} collective-permute-done((bf16[384,512]{1,0:T(8,128)(2,1)S(1)}, bf16[384,512]{1,0:T(8,128)(2,1)S(1)}, u32[]{:S(2)}, u32[]{:S(2)}) %collective-permute-start.16) | collective-permute-done | bytes 393248 | tf_op jit(solution)/shard_map/ppermute | solution.py:48
  (104 shorter events, 72.8 us)
Async XLA Ops:
  7.2 198.8 %all-gather.4.cloned.1.call-start = ((), (), s32[]{:S(2)}) async-start(), calls=%async_computation | async-start | bytes 25952256 | tf_op jit(solution)/shard_map/all_gather | solution.py:78
  10.8 341.9 %all-gather.6.cloned.1.call-start = ((), (), s32[]{:S(2)}) async-start(), calls=%async_computation.1 | async-start | bytes 7077888 | tf_op jit(solution)/shard_map/all_gather | solution.py:85
  13.7 0.7 collective-permute-start.2
  15.3 436.0 %all-gather.8.cloned.1.call-start = ((), (), s32[]{:S(2)}) async-start(), calls=%async_computation.2 | async-start | bytes 7077888 | tf_op jit(solution)/shard_map/all_gather | solution.py:85
  242.8 4.7 collective-permute-start
  245.8 1.5 collective-permute-start.5
  251.9 93.9 %copy-start.10 = (bf16[768,512]{1,0:T(8,128)(2,1)S(1)}, bf16[768,512]{1,0:T(8,128)(2,1)}, u32[]{:S(2)}) copy-start(bf16[768,512]{1,0:T(8,128)(2,1)} %multiply_convert_fusion.2) | copy-start | bytes 2359300
  252.0 92.5 %collective-permute-start.1 = (bf16[1,768,512]{2,1,0:T(8,128)(2,1)S(1)}, bf16[1,768,512]{2,1,0:T(8,128)(2,1)S(1)}, u32[]{:S(2)}, u32[]{:S(2)}) collective-permute-start(bf16[1,768,512]{2,1,0:T(8,128)(2,1)S(1)} %fusion.14), channel_id=1, source_target_pairs={{0,2},{1,3},{2,0},{3,1},{4,6},{5,7},{6,4},{7,5},{8,10},{9,11},{10,... | collective-permute-start | bytes 2359304 | tf_op jit(solution)/shard_map/ppermute | solution.py:20
  389.5 13.1 %collective-permute-start.3 = (bf16[2,768,512]{2,1,0:T(8,128)(2,1)S(1)}, bf16[2,768,512]{2,1,0:T(8,128)(2,1)S(1)}, u32[]{:S(2)}, u32[]{:S(2)}) collective-permute-start(bf16[2,768,512]{2,1,0:T(8,128)(2,1)S(1)} %fusion.9), channel_id=1, source_target_pairs={{0,1},{1,0},{2,3},{3,2},{4,5},{5,4},{6,7},{7,6},{8,9},{9,8},{10,11... | collective-permute-start | bytes 4718600 | tf_op jit(solution)/shard_map/ppermute | solution.py:20
  406.5 21.3 %copy-start.13 = (bf16[768,512]{1,0:T(8,128)(2,1)S(1)}, bf16[768,512]{1,0:T(8,128)(2,1)}, u32[]{:S(2)}) copy-start(bf16[768,512]{1,0:T(8,128)(2,1)} %copy-done.12) | copy-start | bytes 2359300
  406.6 19.9 %collective-permute-start.4 = (bf16[1,768,512]{2,1,0:T(8,128)(2,1)S(1)}, bf16[1,768,512]{2,1,0:T(8,128)(2,1)S(1)}, u32[]{:S(2)}, u32[]{:S(2)}) collective-permute-start(bf16[1,768,512]{2,1,0:T(8,128)(2,1)S(1)} %fusion.15), channel_id=1, source_target_pairs={{0,2},{1,3},{2,0},{3,1},{4,6},{5,7},{6,4},{7,5},{8,10},{9,11},{10,... | collective-permute-start | bytes 2359304 | tf_op jit(solution)/shard_map/ppermute | solution.py:20
  488.0 3.5 collective-permute-start.6
  496.3 19.9 %collective-permute-start.7 = (bf16[1,768,512]{2,1,0:T(8,128)(2,1)}, bf16[1,768,512]{2,1,0:T(8,128)(2,1)}, u32[]{:S(2)}, u32[]{:S(2)}) collective-permute-start(bf16[1,768,512]{2,1,0:T(8,128)(2,1)} %fusion.16), channel_id=1, source_target_pairs={{0,2},{1,3},{2,0},{3,1},{4,6},{5,7},{6,4},{7,5},{8,10},{9,11},{10,... | collective-permute-start | bytes 2359304 | tf_op jit(solution)/shard_map/ppermute | solution.py:20
  497.8 19.8 %copy-start.15 = (bf16[768,512]{1,0:T(8,128)(2,1)S(1)}, bf16[768,512]{1,0:T(8,128)(2,1)}, u32[]{:S(2)}) copy-start(bf16[768,512]{1,0:T(8,128)(2,1)} %copy-done.14) | copy-start | bytes 2359300
  521.6 3.8 collective-permute-start.8
  528.6 19.6 %collective-permute-start.9 = (f32[384,512]{1,0:T(8,128)S(1)}, f32[384,512]{1,0:T(8,128)S(1)}, u32[]{:S(2)}, u32[]{:S(2)}) collective-permute-start(f32[384,512]{1,0:T(8,128)S(1)} %slice_select_fusion.1), channel_id=1, source_target_pairs={{0,2},{1,3},{2,0},{3,1},{4,6},{5,7},{6,4},{7,5},{8,10},{9,11},{10,... | collective-permute-start | bytes 2359304 | tf_op jit(solution)/shard_map/ppermute | solution.py:44
  550.0 10.4 %collective-permute-start.10 = (f32[192,512]{1,0:T(8,128)S(1)}, f32[192,512]{1,0:T(8,128)S(1)}, u32[]{:S(2)}, u32[]{:S(2)}) collective-permute-start(f32[192,512]{1,0:T(8,128)S(1)} %slice_select_fusion.2), channel_id=1, source_target_pairs={{0,4},{1,5},{2,6},{3,7},{4,0},{5,1},{6,2},{7,3},{8,12},{9,13},{10,... | collective-permute-start | bytes 1179656 | tf_op jit(solution)/shard_map/ppermute | solution.py:44
  560.5 5.7 collective-permute-start.11
  566.3 7.4 %collective-permute-start.12 = (f32[48,512]{1,0:T(8,128)S(1)}, f32[48,512]{1,0:T(8,128)S(1)}, u32[]{:S(2)}, u32[]{:S(2)}) collective-permute-start(f32[48,512]{1,0:T(8,128)S(1)} %slice_select_fusion.4), channel_id=1, source_target_pairs={{0,16},{1,17},{2,18},{3,19},{4,20},{5,21},{6,22},{7,23},{8,24},{9,... | collective-permute-start | bytes 294920 | tf_op jit(solution)/shard_map/ppermute | solution.py:44
  573.7 5.1 collective-permute-start.13
  578.8 4.7 collective-permute-start.14
  583.6 5.7 collective-permute-start.15
  589.4 7.8 %collective-permute-start.16 = (bf16[384,512]{1,0:T(8,128)(2,1)S(1)}, bf16[384,512]{1,0:T(8,128)(2,1)S(1)}, u32[]{:S(2)}, u32[]{:S(2)}) collective-permute-start(bf16[384,512]{1,0:T(8,128)(2,1)S(1)} %pad_maximum_fusion.4), channel_id=1, source_target_pairs={{0,2},{1,3},{2,0},{3,1},{4,6},{5,7},{6,4},{7,5},{8,10},{9,11},{10,... | collective-permute-start | bytes 1179656 | tf_op jit(solution)/shard_map/ppermute | solution.py:48
  597.5 2.6 collective-permute-start.17
  (13 other events, 38.1 us)
Sparse Core Ops, SparseCore 0:
  11.4 194.4 all-gather.3
  208.7 144.0 all-gather.5
  354.9 96.2 all-gather.7
